TPU v7x, 128 devices: a whole 4x4x4 slice. The times are simulated.
128 devices in a mesh: mem: 8 (over z_lo, y), sp: 16 (over z_hi, x, core).
Axes of the slice: x: 4, y: 4, z: 4 (z_hi: 2, z_lo: 2; z = z_hi * 2 + z_lo), core: 2. Of those that a mesh axis runs over, the one named last changes fastest.
Arguments:
- anomalies: float32 [64, 3, 256, 4096], P('mem', None, 'sp'), may hold values from -6 to 6
- mean_state: float32 [3, 256, 4096], P(None, 'sp'), may hold values from -3 to 3
- weights: float32 [64], replicated, may hold values from -0.4375 to 0.4375
- station_row: int32 [4096], P('sp'), may hold values from 0 to 14
- station_col: int32 [4096], P('sp'), may hold values from 0 to 4095
- stencil_row: int32 [4, 4096], P(None, 'sp'), may hold values from 0 to 1
- stencil_col: int32 [4, 4096], P(None, 'sp'), may hold values from -1 to 1
- obs_weight: float32 [4, 4096], P(None, 'sp'), may hold values from 0.05 to 0.25
- obs_value: float32 [4, 4096], P(None, 'sp'), may hold values from -6 to 6
- obs_var: float32 [4, 4096], P(None, 'sp'), may hold values from 1 to 10
Outputs:
- obs_anom: float32 [64, 4, 4096], P('mem', None, 'sp')
- gradient: float32 [64], replicated
- hessian: float32 [64, 64], replicated
All inputs are finite; a program needn't handle non-finite values.
Results may differ from a plain program's by a relative error of at most 0.0003.
Values sent between devices are 32-bit elements; how exact they have to be, the bound alone decides.
No kernel may reach another device: no remote copies, remote signals or barrier semaphores. Data moves between devices by JAX's collectives and lax.ppermute only.
A program may use at most 192 MiB of HBM per device.

v0:
```python
import jax
import jax.numpy as jnp
from jax import lax
from jax.sharding import PartitionSpec as P

STEPS = 4
time_step = 1.0
coriolis = 0.1
perturb = 0.1


def padded_2(block, sides, width):
    for axis, dim in sides:
        count = lax.axis_size(axis)
        forward = [(i, i + 1) for i in range(count - 1)]
        forward.append((count - 1, 0))
        backward = [(target, source) for source, target in forward]
        low = lax.ppermute(
            lax.slice_in_dim(block, block.shape[dim] - width, None, axis=dim), axis, forward
        )
        high = lax.ppermute(lax.slice_in_dim(block, 0, width, axis=dim), axis, backward)
        block = jnp.concatenate([low, block, high], axis=dim)
    return block


def row_diff(a):
    return (a[:, 2:] - a[:, :-2]) * 0.5


def col_diff(a):
    return (jnp.roll(a, -1, axis=-1) - jnp.roll(a, 1, axis=-1)) * 0.5


def height_update(height, along, across):
    depth = 1.0 + height
    return height[:, 1:-1] - time_step * (
        row_diff(depth * along) + col_diff(depth * across)[:, 1:-1]
    )


def momentum_update(fresh, along, across):
    inner_u = along[:, 1:-1]
    inner_v = across[:, 1:-1]
    new_u = inner_u + time_step * (
        coriolis * inner_v
        - row_diff(fresh)
        - inner_u * row_diff(along)
        - inner_v * col_diff(along)[:, 1:-1]
    )
    new_v = inner_v + time_step * (
        -coriolis * inner_u
        - col_diff(fresh)[:, 1:-1]
        - inner_u * row_diff(across)
        - inner_v * col_diff(across)[:, 1:-1]
    )
    return jnp.stack([fresh[:, 1:-1], new_u, new_v], axis=1)


def observe(height, flat_index, obs_weight):
    flat = height.reshape(height.shape[0], -1)
    picked = jnp.take(flat, flat_index, axis=1)
    return jnp.sum(obs_weight[None] * picked, axis=1)


def body(
    anomalies,
    mean_state,
    weights,
    station_row,
    station_col,
    stencil_row,
    stencil_col,
    obs_weight,
    obs_value,
    obs_var,
):
    members = anomalies.shape[0]
    columns = anomalies.shape[3]
    total = weights.shape[0]
    first = lax.axis_index("mem") * members
    own_weights = lax.dynamic_slice_in_dim(weights, first, members, 0)
    partial_value = jnp.tensordot(own_weights, anomalies, axes=1, precision=lax.Precision.HIGHEST)
    increment = lax.psum(partial_value, "mem")
    centre = mean_state + increment
    state = centre[None] + perturb * anomalies
    flat_index = (station_row[None, :] + stencil_row) * columns + (
        station_col[None, :] + stencil_col
    ) % columns
    seen = []
    for step in range(STEPS):
        padded = padded_2(state, (("sp", 2),), 1)
        fresh = height_update(padded[:, 0], padded[:, 1], padded[:, 2])
        fresh_pad = padded_2(fresh, (("sp", 1),), 1)
        state = momentum_update(fresh_pad, padded[:, 1], padded[:, 2])
        seen.append(observe(state[:, 0], flat_index, obs_weight))
    own_obs = jnp.stack(seen, axis=1)
    gathered = lax.all_gather(own_obs, "mem", axis=0, tiled=True)
    mean_obs = jnp.mean(gathered, axis=0)
    obs_anom = (own_obs - mean_obs) / perturb
    flat_anom = ((gathered - mean_obs) / perturb).reshape(total, -1)
    weighted = flat_anom * (1.0 / obs_var).reshape(-1)
    innov = (obs_value - mean_obs).reshape(-1)
    gram = jnp.dot(weighted, flat_anom.T, precision=lax.Precision.HIGHEST)
    pull = jnp.dot(weighted, innov, precision=lax.Precision.HIGHEST)
    gram, pull = lax.psum((gram, pull), "sp")
    hessian = gram + (total - 1) * jnp.eye(total, dtype=jnp.float32)
    gradient = (total - 1) * weights - pull
    return (obs_anom, gradient, hessian)


def solution(mesh):
    return jax.shard_map(
        body,
        mesh=mesh,
        in_specs=(
            P("mem", None, "sp", None),
            P(None, "sp", None),
            P(),
            P("sp"),
            P("sp"),
            P(None, "sp"),
            P(None, "sp"),
            P(None, "sp"),
            P(None, "sp"),
            P(None, "sp"),
        ),
        out_specs=(P("mem", None, "sp"), P(), P()),
        check_vma=False,
    )
```

profile of v0, /device:TPU:0, one launch (start us, length us, event | category | flops | bytes accessed | tf_op | source)
XLA Modules:
  0.0 450.2 jit_solution(12270124455747146730)
XLA Ops:
  7.2 11.4 %fusion = f32[1,3,16,4096]{3,0,2,1:T(1,128)S(1)} fusion(f32[8,3,16,4096]{3,2,1,0:T(8,128)} %param.12, f32[64]{0:T(128)} %param.14, s32[]{:T(128)S(6)} %select_n.17), kind=kOutput, calls=%fused_computation.9 | convolution fusion | flops 18874368 | bytes 7078148 | tf_op jit(solution)/shard_map/dot_general | solution.py:82
  20.0 78.6 %all-reduce.3.cloned.1.call-done = f32[3,16,4096]{2,1,0:T(8,128)} async-done(((f32[3,16,4096]{2,1,0:T(8,128)}), f32[3,16,4096]{2,1,0:T(8,128)}) %all-reduce.3.cloned.1.call-update) | async-done | bytes 786448 | tf_op jit(solution)/shard_map/psum | solution.py:83
  99.8 7.0 %multiply_add_fusion = f32[8,3,16,4096]{3,0,2,1:T(8,128)S(1)} fusion(f32[8,3,16,4096]{3,2,1,0:T(8,128)} %param.12, f32[3,16,4096]{2,1,0:T(8,128)S(1)} %add.97), kind=kLoop, calls=%fused_computation.8 | loop fusion | flops 3145728 | bytes 13369344 | tf_op jit(solution)/shard_map/add | solution.py:85
  106.9 5.5 %collective-permute-start.1 = (f32[8,3,1,4096]{3,0,2,1:T(8,128)S(1)}, f32[8,3,1,4096]{3,0,2,1:T(8,128)S(1)}, u32[]{:S(2)}, u32[]{:S(2)}) collective-permute-start(f32[8,3,1,4096]{3,0,2,1:T(8,128)S(1)} %get-tuple-element.42), channel_id=1, source_target_pairs={{1,0},{2,1},{3,2},{4,3},{5,4},{6,5},{7,6},{8,7},{9,8},{10,9},{11,1... | collective-permute-start | bytes 1179656 | tf_op jit(solution)/shard_map/ppermute | solution.py:21
  112.4 5.3 %collective-permute-done = f32[8,3,1,4096]{3,0,2,1:T(8,128)S(1)} collective-permute-done((f32[8,3,1,4096]{3,0,2,1:T(8,128)S(1)}, f32[8,3,1,4096]{3,0,2,1:T(8,128)S(1)}, u32[]{:S(2)}, u32[]{:S(2)}) %collective-permute-start) | collective-permute-done | bytes 393248 | tf_op jit(solution)/shard_map/ppermute | solution.py:18
  121.3 5.6 %collective-permute-start.2 = (f32[8,1,4096]{2,0,1:T(8,128)S(1)}, f32[8,1,4096]{2,0,1:T(8,128)S(1)}, u32[]{:S(2)}, u32[]{:S(2)}) collective-permute-start(f32[8,1,4096]{2,0,1:T(8,128)S(1)} %get-tuple-element.94), channel_id=1, source_target_pairs={{1,0},{2,1},{3,2},{4,3},{5,4},{6,5},{7,6},{8,7},{9,8},{10,9},{11,1... | collective-permute-start | bytes 393224 | tf_op jit(solution)/shard_map/ppermute | solution.py:21
  141.9 5.5 %collective-permute-start.5 = (f32[8,3,1,4096]{3,0,2,1:T(8,128)S(1)}, f32[8,3,1,4096]{3,0,2,1:T(8,128)S(1)}, u32[]{:S(2)}, u32[]{:S(2)}) collective-permute-start(f32[8,3,1,4096]{3,0,2,1:T(8,128)S(1)} %get-tuple-element.40), channel_id=1, source_target_pairs={{1,0},{2,1},{3,2},{4,3},{5,4},{6,5},{7,6},{8,7},{9,8},{10,9},{11,1... | collective-permute-start | bytes 1179656 | tf_op jit(solution)/shard_map/ppermute | solution.py:21
  147.4 5.3 %collective-permute-done.4 = f32[8,3,1,4096]{3,0,2,1:T(8,128)S(1)} collective-permute-done((f32[8,3,1,4096]{3,0,2,1:T(8,128)S(1)}, f32[8,3,1,4096]{3,0,2,1:T(8,128)S(1)}, u32[]{:S(2)}, u32[]{:S(2)}) %collective-permute-start.4) | collective-permute-done | bytes 393248 | tf_op jit(solution)/shard_map/ppermute | solution.py:18
  157.6 5.6 %collective-permute-start.6 = (f32[8,1,4096]{2,0,1:T(8,128)S(1)}, f32[8,1,4096]{2,0,1:T(8,128)S(1)}, u32[]{:S(2)}, u32[]{:S(2)}) collective-permute-start(f32[8,1,4096]{2,0,1:T(8,128)S(1)} %get-tuple-element.92), channel_id=1, source_target_pairs={{1,0},{2,1},{3,2},{4,3},{5,4},{6,5},{7,6},{8,7},{9,8},{10,9},{11,1... | collective-permute-start | bytes 393224 | tf_op jit(solution)/shard_map/ppermute | solution.py:21
  165.7 5.5 %collective-permute-done.7 = f32[8,1,4096]{2,0,1:T(8,128)S(1)} collective-permute-done((f32[8,1,4096]{2,0,1:T(8,128)S(1)}, f32[8,1,4096]{2,0,1:T(8,128)S(1)}, u32[]{:S(2)}, u32[]{:S(2)}) %collective-permute-start.7) | collective-permute-done | bytes 131104 | tf_op jit(solution)/shard_map/ppermute | solution.py:18
  177.4 5.6 %collective-permute-start.9 = (f32[8,3,1,4096]{3,0,2,1:T(8,128)S(1)}, f32[8,3,1,4096]{3,0,2,1:T(8,128)S(1)}, u32[]{:S(2)}, u32[]{:S(2)}) collective-permute-start(f32[8,3,1,4096]{3,0,2,1:T(8,128)S(1)} %get-tuple-element.38), channel_id=1, source_target_pairs={{1,0},{2,1},{3,2},{4,3},{5,4},{6,5},{7,6},{8,7},{9,8},{10,9},{11,1... | collective-permute-start | bytes 1179656 | tf_op jit(solution)/shard_map/ppermute | solution.py:21
  195.2 5.6 %collective-permute-start.10 = (f32[8,1,4096]{2,0,1:T(8,128)S(1)}, f32[8,1,4096]{2,0,1:T(8,128)S(1)}, u32[]{:S(2)}, u32[]{:S(2)}) collective-permute-start(f32[8,1,4096]{2,0,1:T(8,128)S(1)} %get-tuple-element.90), channel_id=1, source_target_pairs={{1,0},{2,1},{3,2},{4,3},{5,4},{6,5},{7,6},{8,7},{9,8},{10,9},{11,1... | collective-permute-start | bytes 393224 | tf_op jit(solution)/shard_map/ppermute | solution.py:21
  203.3 5.5 %collective-permute-done.11 = f32[8,1,4096]{2,0,1:T(8,128)S(1)} collective-permute-done((f32[8,1,4096]{2,0,1:T(8,128)S(1)}, f32[8,1,4096]{2,0,1:T(8,128)S(1)}, u32[]{:S(2)}, u32[]{:S(2)}) %collective-permute-start.11) | collective-permute-done | bytes 131104 | tf_op jit(solution)/shard_map/ppermute | solution.py:18
  216.4 5.6 %collective-permute-start.13 = (f32[8,3,1,4096]{3,0,2,1:T(8,128)}, f32[8,3,1,4096]{3,0,2,1:T(8,128)}, u32[]{:S(2)}, u32[]{:S(2)}) collective-permute-start(f32[8,3,1,4096]{3,0,2,1:T(8,128)} %get-tuple-element.36), channel_id=1, source_target_pairs={{1,0},{2,1},{3,2},{4,3},{5,4},{6,5},{7,6},{8,7},{9,8},{10,9},{11,1... | collective-permute-start | bytes 1179656 | tf_op jit(solution)/shard_map/ppermute | solution.py:21
  222.1 15.6 %copy.29 = f32[8,16,4096]{0,2,1:T(8,128)} copy(f32[8,16,4096]{2,0,1:T(8,128)S(1)} %fusion.94) | data formatting | bytes 4194304 | tf_op jit(solution)/shard_map/sub | solution.py:36
  237.6 13.3 %gather_fusion = f32[1024,8]{1,0:T(8,128)S(1)} fusion(f32[8,65536]{0,1:T(8,128)} %bitcast.122, s32[1024]{0:T(1024)S(1)} %broadcast_clamp_fusion), kind=kCustom, calls=%fused_computation.clone | custom fusion | bytes 69632 | tf_op jit(solution)/shard_map/jit(_take)/gather | solution.py:61
  251.0 16.4 %copy.31 = f32[8,16,4096]{0,2,1:T(8,128)} copy(f32[8,16,4096]{2,0,1:T(8,128)} %copy-done) | data formatting | bytes 4194304 | tf_op jit(solution)/shard_map/sub | solution.py:36
  267.4 13.3 %gather_fusion.1 = f32[1024,8]{1,0:T(8,128)S(1)} fusion(f32[8,65536]{0,1:T(8,128)} %bitcast.123, s32[1024]{0:T(1024)S(1)} %broadcast_clamp_fusion), kind=kCustom, calls=%fused_computation.1.clone | custom fusion | bytes 69632 | tf_op jit(solution)/shard_map/jit(_take)/gather | solution.py:61
  280.8 15.6 %copy.33 = f32[8,16,4096]{0,2,1:T(8,128)} copy(f32[8,16,4096]{2,0,1:T(8,128)S(1)} %copy-done.2) | data formatting | bytes 4194304 | tf_op jit(solution)/shard_map/sub | solution.py:36
  296.3 14.5 %gather_fusion.2 = f32[1024,8]{1,0:T(8,128)} fusion(f32[8,65536]{0,1:T(8,128)} %bitcast.124, s32[1024]{0:T(1024)S(1)} %broadcast_clamp_fusion), kind=kCustom, calls=%fused_computation.2.clone | custom fusion | bytes 69632 | tf_op jit(solution)/shard_map/jit(_take)/gather | solution.py:61
  316.2 15.6 %copy.35 = f32[8,16,4096]{0,2,1:T(8,128)} copy(f32[8,16,4096]{2,0,1:T(8,128)S(1)} %fusion.7) | data formatting | bytes 4194304 | tf_op jit(solution)/shard_map/sub | solution.py:36
  331.8 13.4 %gather_fusion.3 = f32[1024,8]{1,0:T(8,128)S(1)} fusion(f32[8,65536]{0,1:T(8,128)} %bitcast.121, s32[1024]{0:T(1024)S(1)} %broadcast_clamp_fusion), kind=kCustom, calls=%fused_computation.3.clone | custom fusion | bytes 69632 | tf_op jit(solution)/shard_map/jit(_take)/gather | solution.py:61
  346.9 28.4 %all_gather.3 = f32[64,4,256]{2,0,1:T(8,128)S(1)} all-gather(f32[8,4,256]{2,0,1:T(8,128)S(1)} %pad_maximum_fusion.60), channel_id=1, replica_groups=mesh['mem'=8,'sp'=16] {'mem'}, dimensions={0}, use_global_device_ids=true | all-gather | bytes 294912 | tf_op jit(solution)/shard_map/all_gather | solution.py:97
  376.0 65.0 %all-reduce = (f32[64]{0:T(128)S(1)}, f32[64,64]{1,0:T(8,128)S(1)}) all-reduce(f32[64]{0:T(128)S(1)} %convolution_bitcast_fusion.1, f32[64,64]{1,0:T(8,128)S(1)} %convolution_bitcast_fusion), channel_id=1, replica_groups=mesh['mem'=8,'sp'=16] {'sp'}, use_global_device_ids=true, to_apply=%region_6.8 | all-reduce | flops 4160 | bytes 33280 | tf_op jit(solution)/shard_map/psum | solution.py:105
  (124 shorter events, 66.4 us)
Async XLA Ops:
  7.2 91.4 %all-reduce.3.cloned.1.call-start = ((), (), s32[]{:S(2)}) async-start(), calls=%async_computation | async-start | bytes 1572864 | tf_op jit(solution)/shard_map/psum | solution.py:83
  18.6 80.0 %copy-start.7 = (f32[3,16,4096]{2,1,0:T(8,128)S(1)}, f32[3,16,4096]{2,1,0:T(8,128)}, u32[]{:S(2)}) copy-start(f32[3,16,4096]{2,1,0:T(8,128)} %param.13) | copy-start | bytes 2359300
  106.8 10.9 %collective-permute-start = (f32[8,3,1,4096]{3,0,2,1:T(8,128)S(1)}, f32[8,3,1,4096]{3,0,2,1:T(8,128)S(1)}, u32[]{:S(2)}, u32[]{:S(2)}) collective-permute-start(f32[8,3,1,4096]{3,0,2,1:T(8,128)S(1)} %get-tuple-element.41), channel_id=1, source_target_pairs={{0,1},{1,2},{2,3},{3,4},{4,5},{5,6},{6,7},{7,8},{8,9},{9,10},{10,1... | collective-permute-start | bytes 1179656 | tf_op jit(solution)/shard_map/ppermute | solution.py:18
  106.9 10.8 %collective-permute-start.1 = (f32[8,3,1,4096]{3,0,2,1:T(8,128)S(1)}, f32[8,3,1,4096]{3,0,2,1:T(8,128)S(1)}, u32[]{:S(2)}, u32[]{:S(2)}) collective-permute-start(f32[8,3,1,4096]{3,0,2,1:T(8,128)S(1)} %get-tuple-element.42), channel_id=1, source_target_pairs={{1,0},{2,1},{3,2},{4,3},{5,4},{6,5},{7,6},{8,7},{9,8},{10,9},{11,1... | collective-permute-start | bytes 1179656 | tf_op jit(solution)/shard_map/ppermute | solution.py:21
  121.3 8.9 %collective-permute-start.2 = (f32[8,1,4096]{2,0,1:T(8,128)S(1)}, f32[8,1,4096]{2,0,1:T(8,128)S(1)}, u32[]{:S(2)}, u32[]{:S(2)}) collective-permute-start(f32[8,1,4096]{2,0,1:T(8,128)S(1)} %get-tuple-element.94), channel_id=1, source_target_pairs={{1,0},{2,1},{3,2},{4,3},{5,4},{6,5},{7,6},{8,7},{9,8},{10,9},{11,1... | collective-permute-start | bytes 393224 | tf_op jit(solution)/shard_map/ppermute | solution.py:21
  126.8 8.0 %collective-permute-start.3 = (f32[8,1,4096]{2,0,1:T(8,128)S(1)}, f32[8,1,4096]{2,0,1:T(8,128)S(1)}, u32[]{:S(2)}, u32[]{:S(2)}) collective-permute-start(f32[8,1,4096]{2,0,1:T(8,128)S(1)} %get-tuple-element.93), channel_id=1, source_target_pairs={{0,1},{1,2},{2,3},{3,4},{4,5},{5,6},{6,7},{7,8},{8,9},{9,10},{10,1... | collective-permute-start | bytes 393224 | tf_op jit(solution)/shard_map/ppermute | solution.py:18
  141.8 10.9 %collective-permute-start.4 = (f32[8,3,1,4096]{3,0,2,1:T(8,128)S(1)}, f32[8,3,1,4096]{3,0,2,1:T(8,128)S(1)}, u32[]{:S(2)}, u32[]{:S(2)}) collective-permute-start(f32[8,3,1,4096]{3,0,2,1:T(8,128)S(1)} %get-tuple-element.39), channel_id=1, source_target_pairs={{0,1},{1,2},{2,3},{3,4},{4,5},{5,6},{6,7},{7,8},{8,9},{9,10},{10,1... | collective-permute-start | bytes 1179656 | tf_op jit(solution)/shard_map/ppermute | solution.py:18
  141.9 10.8 %collective-permute-start.5 = (f32[8,3,1,4096]{3,0,2,1:T(8,128)S(1)}, f32[8,3,1,4096]{3,0,2,1:T(8,128)S(1)}, u32[]{:S(2)}, u32[]{:S(2)}) collective-permute-start(f32[8,3,1,4096]{3,0,2,1:T(8,128)S(1)} %get-tuple-element.40), channel_id=1, source_target_pairs={{1,0},{2,1},{3,2},{4,3},{5,4},{6,5},{7,6},{8,7},{9,8},{10,9},{11,1... | collective-permute-start | bytes 1179656 | tf_op jit(solution)/shard_map/ppermute | solution.py:21
  157.5 30.8 %copy-start = (f32[8,16,4096]{2,0,1:T(8,128)}, f32[8,16,4096]{2,0,1:T(8,128)S(1)}, u32[]{:S(2)}) copy-start(f32[8,16,4096]{2,0,1:T(8,128)S(1)} %fusion.65) | copy-start | bytes 6291460
  157.6 8.1 %collective-permute-start.6 = (f32[8,1,4096]{2,0,1:T(8,128)S(1)}, f32[8,1,4096]{2,0,1:T(8,128)S(1)}, u32[]{:S(2)}, u32[]{:S(2)}) collective-permute-start(f32[8,1,4096]{2,0,1:T(8,128)S(1)} %get-tuple-element.92), channel_id=1, source_target_pairs={{1,0},{2,1},{3,2},{4,3},{5,4},{6,5},{7,6},{8,7},{9,8},{10,9},{11,1... | collective-permute-start | bytes 393224 | tf_op jit(solution)/shard_map/ppermute | solution.py:21
  163.2 8.0 %collective-permute-start.7 = (f32[8,1,4096]{2,0,1:T(8,128)S(1)}, f32[8,1,4096]{2,0,1:T(8,128)S(1)}, u32[]{:S(2)}, u32[]{:S(2)}) collective-permute-start(f32[8,1,4096]{2,0,1:T(8,128)S(1)} %get-tuple-element.91), channel_id=1, source_target_pairs={{0,1},{1,2},{2,3},{3,4},{4,5},{5,6},{6,7},{7,8},{8,9},{9,10},{10,1... | collective-permute-start | bytes 393224 | tf_op jit(solution)/shard_map/ppermute | solution.py:18
  177.2 5.8 %copy-start.10 = (s32[4,256]{1,0:T(4,128)S(1)}, s32[4,256]{1,0:T(4,128)}, u32[]{:S(2)}) copy-start(s32[4,256]{1,0:T(4,128)} %param.18) | copy-start | bytes 12292
  177.3 10.9 %collective-permute-start.8 = (f32[8,3,1,4096]{3,0,2,1:T(8,128)S(1)}, f32[8,3,1,4096]{3,0,2,1:T(8,128)S(1)}, u32[]{:S(2)}, u32[]{:S(2)}) collective-permute-start(f32[8,3,1,4096]{3,0,2,1:T(8,128)S(1)} %get-tuple-element.37), channel_id=1, source_target_pairs={{0,1},{1,2},{2,3},{3,4},{4,5},{5,6},{6,7},{7,8},{8,9},{9,10},{10,1... | collective-permute-start | bytes 1179656 | tf_op jit(solution)/shard_map/ppermute | solution.py:18
  177.4 10.9 %collective-permute-start.9 = (f32[8,3,1,4096]{3,0,2,1:T(8,128)S(1)}, f32[8,3,1,4096]{3,0,2,1:T(8,128)S(1)}, u32[]{:S(2)}, u32[]{:S(2)}) collective-permute-start(f32[8,3,1,4096]{3,0,2,1:T(8,128)S(1)} %get-tuple-element.38), channel_id=1, source_target_pairs={{1,0},{2,1},{3,2},{4,3},{5,4},{6,5},{7,6},{8,7},{9,8},{10,9},{11,1... | collective-permute-start | bytes 1179656 | tf_op jit(solution)/shard_map/ppermute | solution.py:21
  195.1 19.7 %copy-start.1 = (f32[8,16,4096]{2,0,1:T(8,128)}, f32[8,16,4096]{2,0,1:T(8,128)S(1)}, u32[]{:S(2)}) copy-start(f32[8,16,4096]{2,0,1:T(8,128)S(1)} %fusion.36) | copy-start | bytes 6291460
  195.2 8.1 %collective-permute-start.10 = (f32[8,1,4096]{2,0,1:T(8,128)S(1)}, f32[8,1,4096]{2,0,1:T(8,128)S(1)}, u32[]{:S(2)}, u32[]{:S(2)}) collective-permute-start(f32[8,1,4096]{2,0,1:T(8,128)S(1)} %get-tuple-element.90), channel_id=1, source_target_pairs={{1,0},{2,1},{3,2},{4,3},{5,4},{6,5},{7,6},{8,7},{9,8},{10,9},{11,1... | collective-permute-start | bytes 393224 | tf_op jit(solution)/shard_map/ppermute | solution.py:21
  200.8 8.0 %collective-permute-start.11 = (f32[8,1,4096]{2,0,1:T(8,128)S(1)}, f32[8,1,4096]{2,0,1:T(8,128)S(1)}, u32[]{:S(2)}, u32[]{:S(2)}) collective-permute-start(f32[8,1,4096]{2,0,1:T(8,128)S(1)} %get-tuple-element.89), channel_id=1, source_target_pairs={{0,1},{1,2},{2,3},{3,4},{4,5},{5,6},{6,7},{7,8},{8,9},{9,10},{10,1... | collective-permute-start | bytes 393224 | tf_op jit(solution)/shard_map/ppermute | solution.py:18
  214.9 7.2 %copy-start.9 = (f32[4,256]{1,0:T(4,128)S(1)}, f32[4,256]{1,0:T(4,128)}, u32[]{:S(2)}) copy-start(f32[4,256]{1,0:T(4,128)} %param.21) | copy-start | bytes 12292
  216.4 94.4 %collective-permute-start.12 = (f32[8,3,1,4096]{3,0,2,1:T(8,128)}, f32[8,3,1,4096]{3,0,2,1:T(8,128)S(1)}, u32[]{:S(2)}, u32[]{:S(2)}) collective-permute-start(f32[8,3,1,4096]{3,0,2,1:T(8,128)} %get-tuple-element.35), channel_id=1, source_target_pairs={{0,1},{1,2},{2,3},{3,4},{4,5},{5,6},{6,7},{7,8},{8,9},{9,10},{10,1... | collective-permute-start | bytes 1179656 | tf_op jit(solution)/shard_map/ppermute | solution.py:18
  216.4 94.4 %collective-permute-start.13 = (f32[8,3,1,4096]{3,0,2,1:T(8,128)}, f32[8,3,1,4096]{3,0,2,1:T(8,128)}, u32[]{:S(2)}, u32[]{:S(2)}) collective-permute-start(f32[8,3,1,4096]{3,0,2,1:T(8,128)} %get-tuple-element.36), channel_id=1, source_target_pairs={{1,0},{2,1},{3,2},{4,3},{5,4},{6,5},{7,6},{8,7},{9,8},{10,9},{11,1... | collective-permute-start | bytes 1179656 | tf_op jit(solution)/shard_map/ppermute | solution.py:21
  251.0 29.8 %copy-start.2 = (f32[8,16,4096]{2,0,1:T(8,128)S(1)}, f32[8,16,4096]{2,0,1:T(8,128)}, u32[]{:S(2)}) copy-start(f32[8,16,4096]{2,0,1:T(8,128)} %copy-done.1) | copy-start | bytes 6291460
  316.2 29.0 %copy-start.8 = (f32[4,256]{1,0:T(4,128)S(1)}, f32[4,256]{1,0:T(4,128)}, u32[]{:S(2)}) copy-start(f32[4,256]{1,0:T(4,128)} %param.19) | copy-start | bytes 12292
  331.8 43.5 %copy-start.12 = (f32[4,256]{1,0:T(4,128)S(1)}, f32[4,256]{1,0:T(4,128)}, u32[]{:S(2)}) copy-start(f32[4,256]{1,0:T(4,128)} %param.20) | copy-start | bytes 12292
  345.2 96.5 %copy-start.15 = (f32[64]{0:T(128)S(1)}, f32[64]{0:T(128)}, u32[]{:S(2)}) copy-start(f32[64]{0:T(128)} %param.14) | copy-start | bytes 772
  (7 other events, 25.0 us)
Sparse Core Ops, SparseCore 0:
  20.1 78.3 all-reduce.2
where the time goes:
time: 459 us; the launch traced here: 450 us
  local copies, waits for them, and re-layouts  139 us (30%)
  waiting for transfers between devices  113 us (25%)
  blocking collectives  93.4 us (20%)
  starting transfers between devices  39.3 us (9%)
  other arithmetic  38.2 us (8%)
  between operations  15.1 us (3%)
  matrix products  12 us (3%)
    psum x1, waiting for transfers between devices, body(): increment = lax.psum(partial_value, 'mem')  78.6 us
    psum x1, blocking collectives, body(): gram, pull = lax.psum((gram, pull), 'sp')  65 us
    sub x4, local copies, waits for them, and re-layouts, height_update(): height[:, 1:-1]  63.1 us
    gather x4, local copies, waits for them, and re-layouts, observe(): picked = jnp.take(flat, flat_index, axis=1)  54.6 us
    ppermute x7, starting transfers between devices, padded_2(): lax.ppermute(lax.slice_in_dim(block, 0, width, axis=dim), axis, backward)  39 us
    ppermute x7, waiting for transfers between devices, padded_2(): lax.ppermute(lax.slice_in_dim(block, block.shape[dim] - width, None, axis...  31.4 us
    all_gather x1, blocking collectives, body(): gathered = lax.all_gather(own_obs, 'mem', axis=0, tiled=True)  28.4 us
    another operation x6, other arithmetic, momentum_update(): return jnp.stack([fresh[:, 1:-1], new_u, new_v], axis=1)  15.1 us
  transfers between devices with their start and end apart: 15, of which 10 were waited for; matrix products, arithmetic and copies ran while one was open for 21% of the time, Pallas kernels for 0%

commit v1 on v0

--- a/solution.py
+++ b/solution.py
@@ -1,3 +1,4 @@
+import functools
 import jax
 import jax.numpy as jnp
 from jax import lax
@@ -7,6 +8,21 @@
 time_step = 1.0
 coriolis = 0.1
 perturb = 0.1
+
+
+def spot_pair(xx, peer_axis):
+    return jnp.concatenate(
+        jax.lax.all_to_all(
+            jnp.stack([xx] * jax.lax.axis_size(peer_axis)),
+            axis_name=peer_axis,
+            split_axis=0,
+            concat_axis=0,
+        ),
+        axis=0,
+    )
+
+
+part_sizes = functools.partial(spot_pair, peer_axis="mem")
 
 
 def padded_2(block, sides, width):
@@ -94,7 +110,7 @@
         state = momentum_update(fresh_pad, padded[:, 1], padded[:, 2])
         seen.append(observe(state[:, 0], flat_index, obs_weight))
     own_obs = jnp.stack(seen, axis=1)
-    gathered = lax.all_gather(own_obs, "mem", axis=0, tiled=True)
+    gathered = part_sizes(own_obs)
     mean_obs = jnp.mean(gathered, axis=0)
     obs_anom = (own_obs - mean_obs) / perturb
     flat_anom = ((gathered - mean_obs) / perturb).reshape(total, -1)

time: 459 us -> 439 us (0.956)
  blocking collectives: 93.4 us -> 65 us
  waiting for transfers between devices: 113 us -> 122 us
    all_gather x1 -> x0, blocking collectives: 28.4 us -> none  [body(): gathered = lax.all_gather(own_obs, 'mem', axis=0, tiled=True)]
    all_to_all x0 -> x1, waiting for transfers between devices: none -> 7.27 us  [spot_pair(): jax.lax.all_to_all(jnp.stack([xx] * jax.lax.axis_size(peer_axis)), axis_n...]
  transfers between devices with their start and end apart: 15 -> 16, of which waited for: 10 -> 12; matrix products, arithmetic and copies ran while one was open for 21% -> 22% of each run, Pallas kernels for 0% -> 0%
where the time goes in v1:
time: 439 us; the launch traced here: 431 us
  local copies, waits for them, and re-layouts  135 us (31%)
  waiting for transfers between devices  122 us (28%)
  blocking collectives  65 us (15%)
  starting transfers between devices  42.8 us (10%)
  other arithmetic  38.1 us (9%)
  between operations  15.2 us (3%)
  matrix products  12 us (3%)
    psum x1, waiting for transfers between devices, body(): increment = lax.psum(partial_value, 'mem')  78.6 us
    psum x1, blocking collectives, body(): gram, pull = lax.psum((gram, pull), 'sp')  65 us
    sub x4, local copies, waits for them, and re-layouts, height_update(): height[:, 1:-1]  63.3 us
    gather x4, local copies, waits for them, and re-layouts, observe(): picked = jnp.take(flat, flat_index, axis=1)  54.6 us
    ppermute x7, starting transfers between devices, padded_2(): lax.ppermute(lax.slice_in_dim(block, 0, width, axis=dim), axis, backward)  39 us
    ppermute x7, waiting for transfers between devices, padded_2(): lax.ppermute(lax.slice_in_dim(block, block.shape[dim] - width, None, axis...  32.3 us
    another operation x6, other arithmetic, momentum_update(): return jnp.stack([fresh[:, 1:-1], new_u, new_v], axis=1)  15.1 us
    slice x21, local copies, waits for them, and re-layouts, col_diff(): return (jnp.roll(a, -1, axis=-1) - jnp.roll(a, 1, axis=-1)) * 0.5  11.5 us
  transfers between devices with their start and end apart: 16, of which 12 were waited for; matrix products, arithmetic and copies ran while one was open for 22% of the time, Pallas kernels for 0%

profile of v1, /device:TPU:0, one launch (start us, length us, event | category | flops | bytes accessed | tf_op | source)
XLA Modules:
  0.0 430.7 jit_solution(18393997282913918250)
XLA Ops:
  7.2 11.4 %fusion = f32[1,3,16,4096]{3,0,2,1:T(1,128)S(1)} fusion(f32[8,3,16,4096]{3,2,1,0:T(8,128)} %param.12, f32[64]{0:T(128)} %param.14, s32[]{:T(128)S(6)} %select_n.17), kind=kOutput, calls=%fused_computation.9 | convolution fusion | flops 18874368 | bytes 7078148 | tf_op jit(solution)/shard_map/dot_general | solution.py:98
  20.0 78.6 %all-reduce.3.cloned.1.call-done = f32[3,16,4096]{2,1,0:T(8,128)} async-done(((f32[3,16,4096]{2,1,0:T(8,128)}), f32[3,16,4096]{2,1,0:T(8,128)}) %all-reduce.3.cloned.1.call-update) | async-done | bytes 786448 | tf_op jit(solution)/shard_map/psum | solution.py:99
  99.8 7.0 %multiply_add_fusion = f32[8,3,16,4096]{3,0,2,1:T(8,128)S(1)} fusion(f32[8,3,16,4096]{3,2,1,0:T(8,128)} %param.12, f32[3,16,4096]{2,1,0:T(8,128)S(1)} %add.97), kind=kLoop, calls=%fused_computation.8 | loop fusion | flops 3145728 | bytes 13369344 | tf_op jit(solution)/shard_map/add | solution.py:101
  106.9 5.5 %collective-permute-start.1 = (f32[8,3,1,4096]{3,0,2,1:T(8,128)S(1)}, f32[8,3,1,4096]{3,0,2,1:T(8,128)S(1)}, u32[]{:S(2)}, u32[]{:S(2)}) collective-permute-start(f32[8,3,1,4096]{3,0,2,1:T(8,128)S(1)} %get-tuple-element.45), channel_id=1, source_target_pairs={{1,0},{2,1},{3,2},{4,3},{5,4},{6,5},{7,6},{8,7},{9,8},{10,9},{11,1... | collective-permute-start | bytes 1179656 | tf_op jit(solution)/shard_map/ppermute | solution.py:37
  112.4 5.3 %collective-permute-done = f32[8,3,1,4096]{3,0,2,1:T(8,128)S(1)} collective-permute-done((f32[8,3,1,4096]{3,0,2,1:T(8,128)S(1)}, f32[8,3,1,4096]{3,0,2,1:T(8,128)S(1)}, u32[]{:S(2)}, u32[]{:S(2)}) %collective-permute-start) | collective-permute-done | bytes 393248 | tf_op jit(solution)/shard_map/ppermute | solution.py:34
  121.3 5.6 %collective-permute-start.2 = (f32[8,1,4096]{2,0,1:T(8,128)S(1)}, f32[8,1,4096]{2,0,1:T(8,128)S(1)}, u32[]{:S(2)}, u32[]{:S(2)}) collective-permute-start(f32[8,1,4096]{2,0,1:T(8,128)S(1)} %get-tuple-element.97), channel_id=1, source_target_pairs={{1,0},{2,1},{3,2},{4,3},{5,4},{6,5},{7,6},{8,7},{9,8},{10,9},{11,1... | collective-permute-start | bytes 393224 | tf_op jit(solution)/shard_map/ppermute | solution.py:37
  129.4 5.5 %collective-permute-done.3 = f32[8,1,4096]{2,0,1:T(8,128)S(1)} collective-permute-done((f32[8,1,4096]{2,0,1:T(8,128)S(1)}, f32[8,1,4096]{2,0,1:T(8,128)S(1)}, u32[]{:S(2)}, u32[]{:S(2)}) %collective-permute-start.3) | collective-permute-done | bytes 131104 | tf_op jit(solution)/shard_map/ppermute | solution.py:34
  141.1 5.5 %collective-permute-start.5 = (f32[8,3,1,4096]{3,0,2,1:T(8,128)S(1)}, f32[8,3,1,4096]{3,0,2,1:T(8,128)S(1)}, u32[]{:S(2)}, u32[]{:S(2)}) collective-permute-start(f32[8,3,1,4096]{3,0,2,1:T(8,128)S(1)} %get-tuple-element.43), channel_id=1, source_target_pairs={{1,0},{2,1},{3,2},{4,3},{5,4},{6,5},{7,6},{8,7},{9,8},{10,9},{11,1... | collective-permute-start | bytes 1179656 | tf_op jit(solution)/shard_map/ppermute | solution.py:37
  156.7 5.6 %collective-permute-start.6 = (f32[8,1,4096]{2,0,1:T(8,128)S(1)}, f32[8,1,4096]{2,0,1:T(8,128)S(1)}, u32[]{:S(2)}, u32[]{:S(2)}) collective-permute-start(f32[8,1,4096]{2,0,1:T(8,128)S(1)} %get-tuple-element.95), channel_id=1, source_target_pairs={{1,0},{2,1},{3,2},{4,3},{5,4},{6,5},{7,6},{8,7},{9,8},{10,9},{11,1... | collective-permute-start | bytes 393224 | tf_op jit(solution)/shard_map/ppermute | solution.py:37
  164.8 5.5 %collective-permute-done.7 = f32[8,1,4096]{2,0,1:T(8,128)S(1)} collective-permute-done((f32[8,1,4096]{2,0,1:T(8,128)S(1)}, f32[8,1,4096]{2,0,1:T(8,128)S(1)}, u32[]{:S(2)}, u32[]{:S(2)}) %collective-permute-start.7) | collective-permute-done | bytes 131104 | tf_op jit(solution)/shard_map/ppermute | solution.py:34
  176.5 5.6 %collective-permute-start.9 = (f32[8,3,1,4096]{3,0,2,1:T(8,128)S(1)}, f32[8,3,1,4096]{3,0,2,1:T(8,128)S(1)}, u32[]{:S(2)}, u32[]{:S(2)}) collective-permute-start(f32[8,3,1,4096]{3,0,2,1:T(8,128)S(1)} %get-tuple-element.41), channel_id=1, source_target_pairs={{1,0},{2,1},{3,2},{4,3},{5,4},{6,5},{7,6},{8,7},{9,8},{10,9},{11,1... | collective-permute-start | bytes 1179656 | tf_op jit(solution)/shard_map/ppermute | solution.py:37
  192.2 5.6 %collective-permute-start.10 = (f32[8,1,4096]{2,0,1:T(8,128)S(1)}, f32[8,1,4096]{2,0,1:T(8,128)S(1)}, u32[]{:S(2)}, u32[]{:S(2)}) collective-permute-start(f32[8,1,4096]{2,0,1:T(8,128)S(1)} %get-tuple-element.93), channel_id=1, source_target_pairs={{1,0},{2,1},{3,2},{4,3},{5,4},{6,5},{7,6},{8,7},{9,8},{10,9},{11,1... | collective-permute-start | bytes 393224 | tf_op jit(solution)/shard_map/ppermute | solution.py:37
  200.3 5.5 %collective-permute-done.11 = f32[8,1,4096]{2,0,1:T(8,128)S(1)} collective-permute-done((f32[8,1,4096]{2,0,1:T(8,128)S(1)}, f32[8,1,4096]{2,0,1:T(8,128)S(1)}, u32[]{:S(2)}, u32[]{:S(2)}) %collective-permute-start.11) | collective-permute-done | bytes 131104 | tf_op jit(solution)/shard_map/ppermute | solution.py:34
  213.4 5.6 %collective-permute-start.13 = (f32[8,3,1,4096]{3,0,2,1:T(8,128)}, f32[8,3,1,4096]{3,0,2,1:T(8,128)}, u32[]{:S(2)}, u32[]{:S(2)}) collective-permute-start(f32[8,3,1,4096]{3,0,2,1:T(8,128)} %get-tuple-element.39), channel_id=1, source_target_pairs={{1,0},{2,1},{3,2},{4,3},{5,4},{6,5},{7,6},{8,7},{9,8},{10,9},{11,1... | collective-permute-start | bytes 1179656 | tf_op jit(solution)/shard_map/ppermute | solution.py:37
  219.1 15.6 %copy.39 = f32[8,16,4096]{0,2,1:T(8,128)} copy(f32[8,16,4096]{2,0,1:T(8,128)S(1)} %fusion.94) | data formatting | bytes 4194304 | tf_op jit(solution)/shard_map/sub | solution.py:52
  234.7 13.3 %gather_fusion = f32[1024,8]{1,0:T(8,128)S(1)} fusion(f32[8,65536]{0,1:T(8,128)} %bitcast.129, s32[1024]{0:T(1024)S(1)} %broadcast_clamp_fusion), kind=kCustom, calls=%fused_computation.clone | custom fusion | bytes 69632 | tf_op jit(solution)/shard_map/jit(_take)/gather | solution.py:77
  248.1 16.5 %copy.41 = f32[8,16,4096]{0,2,1:T(8,128)} copy(f32[8,16,4096]{2,0,1:T(8,128)} %copy-done) | data formatting | bytes 4194304 | tf_op jit(solution)/shard_map/sub | solution.py:52
  264.6 13.3 %gather_fusion.1 = f32[1024,8]{1,0:T(8,128)S(1)} fusion(f32[8,65536]{0,1:T(8,128)} %bitcast.130, s32[1024]{0:T(1024)S(1)} %broadcast_clamp_fusion), kind=kCustom, calls=%fused_computation.1.clone | custom fusion | bytes 69632 | tf_op jit(solution)/shard_map/jit(_take)/gather | solution.py:77
  277.9 15.6 %copy.43 = f32[8,16,4096]{0,2,1:T(8,128)} copy(f32[8,16,4096]{2,0,1:T(8,128)S(1)} %copy-done.2) | data formatting | bytes 4194304 | tf_op jit(solution)/shard_map/sub | solution.py:52
  293.5 14.6 %gather_fusion.2 = f32[1024,8]{1,0:T(8,128)} fusion(f32[8,65536]{0,1:T(8,128)} %bitcast.131, s32[1024]{0:T(1024)S(1)} %broadcast_clamp_fusion), kind=kCustom, calls=%fused_computation.2.clone | custom fusion | bytes 69632 | tf_op jit(solution)/shard_map/jit(_take)/gather | solution.py:77
  313.5 15.6 %copy.45 = f32[8,16,4096]{0,2,1:T(8,128)} copy(f32[8,16,4096]{2,0,1:T(8,128)S(1)} %fusion.7) | data formatting | bytes 4194304 | tf_op jit(solution)/shard_map/sub | solution.py:52
  329.1 13.3 %gather_fusion.3 = f32[1024,8]{1,0:T(8,128)S(1)} fusion(f32[8,65536]{0,1:T(8,128)} %bitcast.128, s32[1024]{0:T(1024)S(1)} %broadcast_clamp_fusion), kind=kCustom, calls=%fused_computation.3.clone | custom fusion | bytes 69632 | tf_op jit(solution)/shard_map/jit(_take)/gather | solution.py:77
  348.5 7.3 %all-to-all-done = f32[8,8,4,256]{3,1,2,0:T(8,128)S(1)} async-done(((f32[8,8,4,256]{3,1,2,0:T(8,128)}), f32[8,8,4,256]{3,1,2,0:T(8,128)S(1)}, u32[]{:S(2)}, u32[]{:S(2)}) %all-to-all-start) | async-done | bytes 262176 | tf_op jit(solution)/shard_map/all_to_all | solution.py:15
  356.5 65.0 %all-reduce = (f32[64]{0:T(128)S(1)}, f32[64,64]{1,0:T(8,128)S(1)}) all-reduce(f32[64]{0:T(128)S(1)} %convolution_bitcast_fusion, f32[64,64]{1,0:T(8,128)S(1)} %fusion.131), channel_id=1, replica_groups=mesh['mem'=8,'sp'=16] {'sp'}, use_global_device_ids=true, to_apply=%region_6.8 | all-reduce | flops 4160 | bytes 33280 | tf_op jit(solution)/shard_map/psum | solution.py:121
  (124 shorter events, 67.6 us)
Async XLA Ops:
  7.2 91.4 %all-reduce.3.cloned.1.call-start = ((), (), s32[]{:S(2)}) async-start(), calls=%async_computation.1 | async-start | bytes 1572864 | tf_op jit(solution)/shard_map/psum | solution.py:99
  18.6 80.0 %copy-start.5 = (f32[3,16,4096]{2,1,0:T(8,128)S(1)}, f32[3,16,4096]{2,1,0:T(8,128)}, u32[]{:S(2)}) copy-start(f32[3,16,4096]{2,1,0:T(8,128)} %param.13) | copy-start | bytes 2359300
  106.8 10.9 %collective-permute-start = (f32[8,3,1,4096]{3,0,2,1:T(8,128)S(1)}, f32[8,3,1,4096]{3,0,2,1:T(8,128)S(1)}, u32[]{:S(2)}, u32[]{:S(2)}) collective-permute-start(f32[8,3,1,4096]{3,0,2,1:T(8,128)S(1)} %get-tuple-element.44), channel_id=1, source_target_pairs={{0,1},{1,2},{2,3},{3,4},{4,5},{5,6},{6,7},{7,8},{8,9},{9,10},{10,1... | collective-permute-start | bytes 1179656 | tf_op jit(solution)/shard_map/ppermute | solution.py:34
  106.9 10.8 %collective-permute-start.1 = (f32[8,3,1,4096]{3,0,2,1:T(8,128)S(1)}, f32[8,3,1,4096]{3,0,2,1:T(8,128)S(1)}, u32[]{:S(2)}, u32[]{:S(2)}) collective-permute-start(f32[8,3,1,4096]{3,0,2,1:T(8,128)S(1)} %get-tuple-element.45), channel_id=1, source_target_pairs={{1,0},{2,1},{3,2},{4,3},{5,4},{6,5},{7,6},{8,7},{9,8},{10,9},{11,1... | collective-permute-start | bytes 1179656 | tf_op jit(solution)/shard_map/ppermute | solution.py:37
  121.3 8.1 %collective-permute-start.2 = (f32[8,1,4096]{2,0,1:T(8,128)S(1)}, f32[8,1,4096]{2,0,1:T(8,128)S(1)}, u32[]{:S(2)}, u32[]{:S(2)}) collective-permute-start(f32[8,1,4096]{2,0,1:T(8,128)S(1)} %get-tuple-element.97), channel_id=1, source_target_pairs={{1,0},{2,1},{3,2},{4,3},{5,4},{6,5},{7,6},{8,7},{9,8},{10,9},{11,1... | collective-permute-start | bytes 393224 | tf_op jit(solution)/shard_map/ppermute | solution.py:37
  126.8 8.0 %collective-permute-start.3 = (f32[8,1,4096]{2,0,1:T(8,128)S(1)}, f32[8,1,4096]{2,0,1:T(8,128)S(1)}, u32[]{:S(2)}, u32[]{:S(2)}) collective-permute-start(f32[8,1,4096]{2,0,1:T(8,128)S(1)} %get-tuple-element.96), channel_id=1, source_target_pairs={{0,1},{1,2},{2,3},{3,4},{4,5},{5,6},{6,7},{7,8},{8,9},{9,10},{10,1... | collective-permute-start | bytes 393224 | tf_op jit(solution)/shard_map/ppermute | solution.py:34
  141.0 10.9 %collective-permute-start.4 = (f32[8,3,1,4096]{3,0,2,1:T(8,128)S(1)}, f32[8,3,1,4096]{3,0,2,1:T(8,128)S(1)}, u32[]{:S(2)}, u32[]{:S(2)}) collective-permute-start(f32[8,3,1,4096]{3,0,2,1:T(8,128)S(1)} %get-tuple-element.42), channel_id=1, source_target_pairs={{0,1},{1,2},{2,3},{3,4},{4,5},{5,6},{6,7},{7,8},{8,9},{9,10},{10,1... | collective-permute-start | bytes 1179656 | tf_op jit(solution)/shard_map/ppermute | solution.py:34
  141.1 10.8 %collective-permute-start.5 = (f32[8,3,1,4096]{3,0,2,1:T(8,128)S(1)}, f32[8,3,1,4096]{3,0,2,1:T(8,128)S(1)}, u32[]{:S(2)}, u32[]{:S(2)}) collective-permute-start(f32[8,3,1,4096]{3,0,2,1:T(8,128)S(1)} %get-tuple-element.43), channel_id=1, source_target_pairs={{1,0},{2,1},{3,2},{4,3},{5,4},{6,5},{7,6},{8,7},{9,8},{10,9},{11,1... | collective-permute-start | bytes 1179656 | tf_op jit(solution)/shard_map/ppermute | solution.py:37
  156.6 30.7 %copy-start = (f32[8,16,4096]{2,0,1:T(8,128)}, f32[8,16,4096]{2,0,1:T(8,128)S(1)}, u32[]{:S(2)}) copy-start(f32[8,16,4096]{2,0,1:T(8,128)S(1)} %fusion.65) | copy-start | bytes 6291460
  156.7 8.1 %collective-permute-start.6 = (f32[8,1,4096]{2,0,1:T(8,128)S(1)}, f32[8,1,4096]{2,0,1:T(8,128)S(1)}, u32[]{:S(2)}, u32[]{:S(2)}) collective-permute-start(f32[8,1,4096]{2,0,1:T(8,128)S(1)} %get-tuple-element.95), channel_id=1, source_target_pairs={{1,0},{2,1},{3,2},{4,3},{5,4},{6,5},{7,6},{8,7},{9,8},{10,9},{11,1... | collective-permute-start | bytes 393224 | tf_op jit(solution)/shard_map/ppermute | solution.py:37
  162.3 8.0 %collective-permute-start.7 = (f32[8,1,4096]{2,0,1:T(8,128)S(1)}, f32[8,1,4096]{2,0,1:T(8,128)S(1)}, u32[]{:S(2)}, u32[]{:S(2)}) collective-permute-start(f32[8,1,4096]{2,0,1:T(8,128)S(1)} %get-tuple-element.94), channel_id=1, source_target_pairs={{0,1},{1,2},{2,3},{3,4},{4,5},{5,6},{6,7},{7,8},{8,9},{9,10},{10,1... | collective-permute-start | bytes 393224 | tf_op jit(solution)/shard_map/ppermute | solution.py:34
  176.4 10.9 %collective-permute-start.8 = (f32[8,3,1,4096]{3,0,2,1:T(8,128)S(1)}, f32[8,3,1,4096]{3,0,2,1:T(8,128)S(1)}, u32[]{:S(2)}, u32[]{:S(2)}) collective-permute-start(f32[8,3,1,4096]{3,0,2,1:T(8,128)S(1)} %get-tuple-element.40), channel_id=1, source_target_pairs={{0,1},{1,2},{2,3},{3,4},{4,5},{5,6},{6,7},{7,8},{8,9},{9,10},{10,1... | collective-permute-start | bytes 1179656 | tf_op jit(solution)/shard_map/ppermute | solution.py:34
  176.5 10.9 %collective-permute-start.9 = (f32[8,3,1,4096]{3,0,2,1:T(8,128)S(1)}, f32[8,3,1,4096]{3,0,2,1:T(8,128)S(1)}, u32[]{:S(2)}, u32[]{:S(2)}) collective-permute-start(f32[8,3,1,4096]{3,0,2,1:T(8,128)S(1)} %get-tuple-element.41), channel_id=1, source_target_pairs={{1,0},{2,1},{3,2},{4,3},{5,4},{6,5},{7,6},{8,7},{9,8},{10,9},{11,1... | collective-permute-start | bytes 1179656 | tf_op jit(solution)/shard_map/ppermute | solution.py:37
  192.1 19.7 %copy-start.1 = (f32[8,16,4096]{2,0,1:T(8,128)}, f32[8,16,4096]{2,0,1:T(8,128)S(1)}, u32[]{:S(2)}) copy-start(f32[8,16,4096]{2,0,1:T(8,128)S(1)} %fusion.36) | copy-start | bytes 6291460
  192.2 8.1 %collective-permute-start.10 = (f32[8,1,4096]{2,0,1:T(8,128)S(1)}, f32[8,1,4096]{2,0,1:T(8,128)S(1)}, u32[]{:S(2)}, u32[]{:S(2)}) collective-permute-start(f32[8,1,4096]{2,0,1:T(8,128)S(1)} %get-tuple-element.93), channel_id=1, source_target_pairs={{1,0},{2,1},{3,2},{4,3},{5,4},{6,5},{7,6},{8,7},{9,8},{10,9},{11,1... | collective-permute-start | bytes 393224 | tf_op jit(solution)/shard_map/ppermute | solution.py:37
  197.8 8.0 %collective-permute-start.11 = (f32[8,1,4096]{2,0,1:T(8,128)S(1)}, f32[8,1,4096]{2,0,1:T(8,128)S(1)}, u32[]{:S(2)}, u32[]{:S(2)}) collective-permute-start(f32[8,1,4096]{2,0,1:T(8,128)S(1)} %get-tuple-element.92), channel_id=1, source_target_pairs={{0,1},{1,2},{2,3},{3,4},{4,5},{5,6},{6,7},{7,8},{8,9},{9,10},{10,1... | collective-permute-start | bytes 393224 | tf_op jit(solution)/shard_map/ppermute | solution.py:34
  211.9 7.2 %copy-start.8 = (s32[4,256]{1,0:T(4,128)S(1)}, s32[4,256]{1,0:T(4,128)}, u32[]{:S(2)}) copy-start(s32[4,256]{1,0:T(4,128)} %param.18) | copy-start | bytes 12292
  213.4 94.7 %collective-permute-start.12 = (f32[8,3,1,4096]{3,0,2,1:T(8,128)}, f32[8,3,1,4096]{3,0,2,1:T(8,128)S(1)}, u32[]{:S(2)}, u32[]{:S(2)}) collective-permute-start(f32[8,3,1,4096]{3,0,2,1:T(8,128)} %get-tuple-element.38), channel_id=1, source_target_pairs={{0,1},{1,2},{2,3},{3,4},{4,5},{5,6},{6,7},{7,8},{8,9},{9,10},{10,1... | collective-permute-start | bytes 1179656 | tf_op jit(solution)/shard_map/ppermute | solution.py:34
  213.4 94.7 %collective-permute-start.13 = (f32[8,3,1,4096]{3,0,2,1:T(8,128)}, f32[8,3,1,4096]{3,0,2,1:T(8,128)}, u32[]{:S(2)}, u32[]{:S(2)}) collective-permute-start(f32[8,3,1,4096]{3,0,2,1:T(8,128)} %get-tuple-element.39), channel_id=1, source_target_pairs={{1,0},{2,1},{3,2},{4,3},{5,4},{6,5},{7,6},{8,7},{9,8},{10,9},{11,1... | collective-permute-start | bytes 1179656 | tf_op jit(solution)/shard_map/ppermute | solution.py:37
  248.1 29.8 %copy-start.2 = (f32[8,16,4096]{2,0,1:T(8,128)S(1)}, f32[8,16,4096]{2,0,1:T(8,128)}, u32[]{:S(2)}) copy-start(f32[8,16,4096]{2,0,1:T(8,128)} %copy-done.1) | copy-start | bytes 6291460
  313.4 29.0 %copy-start.6 = (f32[4,256]{1,0:T(4,128)S(1)}, f32[4,256]{1,0:T(4,128)}, u32[]{:S(2)}) copy-start(f32[4,256]{1,0:T(4,128)} %param.19) | copy-start | bytes 12292
  342.5 13.3 %copy-start.10 = (f32[4,256]{1,0:T(4,128)S(1)}, f32[4,256]{1,0:T(4,128)}, u32[]{:S(2)}) copy-start(f32[4,256]{1,0:T(4,128)} %param.20) | copy-start | bytes 12292
  343.9 78.3 %copy-start.13 = (f32[64]{0:T(128)S(1)}, f32[64]{0:T(128)}, u32[]{:S(2)}) copy-start(f32[64]{0:T(128)} %param.14) | copy-start | bytes 772
  344.9 10.8 %all-to-all-start = ((f32[8,8,4,256]{3,1,2,0:T(8,128)}), f32[8,8,4,256]{3,1,2,0:T(8,128)S(1)}, u32[]{:S(2)}, u32[]{:S(2)}) async-start(f32[8,8,4,256]{3,1,2,0:T(8,128)} %stack.79), calls=%async_computation | async-start | bytes 524288 | tf_op jit(solution)/shard_map/all_to_all | solution.py:15
  (6 other events, 32.0 us)
Sparse Core Ops, SparseCore 0:
  20.1 78.3 all-reduce.2
